TPU v7x, 256 devices: a whole 4x4x8 slice. The times are simulated.
256 devices in a mesh: row: 16 (over z, core), col: 4 (over x), rhs: 4 (over y).
Axes of the slice: x: 4, y: 4, z: 8, core: 2. Of those that a mesh axis runs over, the one named last changes fastest.
Arguments:
- factor: bfloat16 [32768, 8192], P('row', 'col'), may hold values from -0.0625 to 0.0625
- samples: float32 [32768, 512], P('row', 'rhs'), may hold values from -6 to 6
- inverses: bfloat16 [8, 1024, 1024], P(None, 'row', 'col'), may hold values from -0.1875 to 0.1875
Outputs:
- solution: bfloat16 [8, 1024, 512], P(None, 'col', 'rhs')
- remaining: float32 [32768, 512], P(('row', 'col'), 'rhs')
All inputs are finite; a program needn't handle non-finite values.
Results may differ from a plain program's by a relative error of at most 0.006.
Values may be sent and summed in bfloat16 or wider, within the bound.
No kernel may reach another device: no remote copies, remote signals or barrier semaphores. Data moves between devices by JAX's collectives and lax.ppermute only.
A program may use at most 64 MiB of HBM per device.

v0:
```python
import jax
import jax.numpy as jnp
from jax import lax
from jax.sharding import PartitionSpec as P


def from_root(value, axis, source):
    kept = jnp.where(lax.axis_index(axis) == source, value, 0).astype(value.dtype)
    return lax.psum(kept, axis)


def shards(factor, samples, inverses):
    row_total = lax.axis_size("row")
    col_total = lax.axis_size("col")
    row_index = lax.axis_index("row")
    col_index = lax.axis_index("col")
    diag_count = inverses.shape[0]
    width = inverses.shape[1] * row_total
    part_rows = width // col_total
    row_slots = factor.shape[0] // width
    sample_cols = samples.shape[1]
    rhs_blocks = samples.reshape(row_slots, width, sample_cols)
    partial_value = jnp.zeros((row_slots, width, sample_cols), jnp.float32)
    factor_rows = jnp.arange(row_slots, dtype=jnp.int32) * row_total + row_index
    lower_mask = (
        jnp.arange(width)[:, None] >= col_index * part_rows + jnp.arange(part_rows)[None, :]
    )
    solutions = []
    for block in range(diag_count):
        owner_row = block % row_total
        slot_index = block // row_total
        inverse_cols_part = lax.all_gather(inverses[block], "row", axis=0, tiled=True)
        reduced = lax.psum_scatter(
            partial_value[slot_index], "col", scatter_dimension=0, tiled=True
        )
        own_rhs = lax.dynamic_slice_in_dim(
            rhs_blocks[slot_index], col_index * part_rows, part_rows, 0
        )
        lowered = (own_rhs - reduced).astype(jnp.bfloat16)
        inverse_part = jnp.where(lower_mask, inverse_cols_part, jnp.zeros((), jnp.bfloat16))

        def solve_term(row_start, row_count, inverse_part=inverse_part, lowered=lowered):
            return jnp.dot(inverse_part, lowered, preferred_element_type=jnp.float32)

        solved_rows = lax.psum_scatter(
            solve_term(jnp.int32(0), lax.axis_size("col") * part_rows),
            "col",
            scatter_dimension=0,
            tiled=True,
        ).astype(jnp.bfloat16)
        solved_full = lax.all_gather(solved_rows, "col", axis=0, tiled=True)
        solved_full = from_root(solved_full, "row", owner_row)
        solved_part = lax.dynamic_slice_in_dim(solved_full, col_index * part_rows, part_rows, 0)
        solutions.append(solved_part)
        col_slot = block // col_total
        column = factor[:, col_slot * width : (col_slot + 1) * width]
        keep_rows = factor_rows > block

        def apply_update(current, column=column, solved_full=solved_full, keep_rows=keep_rows):
            update = jnp.dot(column, solved_full, preferred_element_type=jnp.float32).reshape(
                row_slots, width, sample_cols
            )
            return current + jnp.where(keep_rows[:, None, None], update, jnp.float32(0.0))

        def unchanged(current):
            return current

        partial_value = lax.cond(
            col_index == block % col_total, apply_update, unchanged, partial_value
        )
    remain = lax.psum_scatter(
        partial_value.reshape(row_slots * width, sample_cols).astype(jnp.bfloat16),
        "col",
        scatter_dimension=0,
        tiled=True,
    ).astype(jnp.float32)
    out_rows = row_slots * width // col_total
    own_rows = lax.dynamic_slice_in_dim(samples, col_index * out_rows, out_rows, 0)
    return (jnp.stack(solutions), own_rows - remain)


def solution(mesh):
    in_specs = (P("row", "col"), P("row", "rhs"), P(None, "row", "col"))
    out_specs = (P(None, "col", "rhs"), P(("row", "col"), "rhs"))
    return jax.shard_map(shards, mesh=mesh, in_specs=in_specs, out_specs=out_specs, check_vma=False)
```

profile of v0, /device:TPU:8, one launch (start us, length us, event | category | flops | bytes accessed | tf_op | source)
XLA Modules:
  0.0 1471.2 jit_solution(4502672935829029276)
XLA Ops:
  8.1 21.4 %all-gather = bf16[1,1024,256]{2,1,0:T(8,128)(2,1)S(1)} all-gather(bf16[1,64,256]{2,1,0:T(8,128)(2,1)S(1)} %get-tuple-element.158), channel_id=2, replica_groups=mesh['row'=16,'col'=4,'rhs'=4] {'row'}, dimensions={1}, use_global_device_ids=true | all-gather | bytes 557056 | tf_op jit(solution)/shard_map/all_gather | solution.py:32
  31.8 22.3 %reduce-scatter.17.cloned.1.call-done = f32[256,128]{1,0:T(8,128)} async-done(((f32[1024,128]{1,0:T(8,128)}), f32[256,128]{1,0:T(8,128)}) %reduce-scatter.17.cloned.1.call-update) | async-done | bytes 131088 | tf_op jit(solution)/shard_map/reduce_scatter | solution.py:45
  55.0 12.2 all_gather.49
  68.1 5.9 fusion.64
  74.0 103.9 %all-reduce.9.cloned.1.call-done = bf16[1024,128]{1,0:T(8,128)(2,1)} async-done(((bf16[1024,128]{1,0:T(8,128)(2,1)}), bf16[1024,128]{1,0:T(8,128)(2,1)}) %all-reduce.9.cloned.1.call-update) | async-done | bytes 262160 | tf_op jit(solution)/shard_map/psum | solution.py:9
  177.9 3.6 conditional.8
  177.9 3.5 fusion.66
  182.4 16.6 %all-gather.1 = bf16[1,1024,256]{2,1,0:T(8,128)(2,1)S(1)} all-gather(bf16[1,64,256]{2,1,0:T(8,128)(2,1)S(1)} %get-tuple-element.157), channel_id=3, replica_groups=mesh['row'=16,'col'=4,'rhs'=4] {'row'}, dimensions={1}, use_global_device_ids=true | all-gather | bytes 557056 | tf_op jit(solution)/shard_map/all_gather | solution.py:32
  199.0 6.6 reduce-scatter.19.cloned.1.call-done
  207.7 25.0 %reduce-scatter.21.cloned.1.call-done = f32[256,128]{1,0:T(8,128)} async-done(((f32[1024,128]{1,0:T(8,128)}), f32[256,128]{1,0:T(8,128)}) %reduce-scatter.21.cloned.1.call-update) | async-done | bytes 131088 | tf_op jit(solution)/shard_map/reduce_scatter | solution.py:45
  233.6 12.2 all_gather.51
  246.6 109.8 %all-reduce.11.cloned.1.call-done = bf16[1024,128]{1,0:T(8,128)(2,1)} async-done(((bf16[1024,128]{1,0:T(8,128)(2,1)}), bf16[1024,128]{1,0:T(8,128)(2,1)}) %all-reduce.11.cloned.1.call-update) | async-done | bytes 262160 | tf_op jit(solution)/shard_map/psum | solution.py:9
  357.4 16.5 %all-gather.2 = bf16[1,1024,256]{2,1,0:T(8,128)(2,1)S(1)} all-gather(bf16[1,64,256]{2,1,0:T(8,128)(2,1)S(1)} %get-tuple-element.156), channel_id=4, replica_groups=mesh['row'=16,'col'=4,'rhs'=4] {'row'}, dimensions={1}, use_global_device_ids=true | all-gather | bytes 557056 | tf_op jit(solution)/shard_map/all_gather | solution.py:32
  373.9 10.6 reduce-scatter.23.cloned.1.call-done
  384.5 2.0 fusion.12
  386.6 25.0 %reduce-scatter.25.cloned.1.call-done = f32[256,128]{1,0:T(8,128)} async-done(((f32[1024,128]{1,0:T(8,128)}), f32[256,128]{1,0:T(8,128)}) %reduce-scatter.25.cloned.1.call-update) | async-done | bytes 131088 | tf_op jit(solution)/shard_map/reduce_scatter | solution.py:45
  412.5 12.2 all_gather.53
  425.5 109.9 %all-reduce.13.cloned.1.call-done = bf16[1024,128]{1,0:T(8,128)(2,1)} async-done(((bf16[1024,128]{1,0:T(8,128)(2,1)}), bf16[1024,128]{1,0:T(8,128)(2,1)}) %all-reduce.13.cloned.1.call-update) | async-done | bytes 262160 | tf_op jit(solution)/shard_map/psum | solution.py:9
  536.3 16.5 %all-gather.3 = bf16[1,1024,256]{2,1,0:T(8,128)(2,1)S(1)} all-gather(bf16[1,64,256]{2,1,0:T(8,128)(2,1)S(1)} %get-tuple-element.155), channel_id=5, replica_groups=mesh['row'=16,'col'=4,'rhs'=4] {'row'}, dimensions={1}, use_global_device_ids=true | all-gather | bytes 557056 | tf_op jit(solution)/shard_map/all_gather | solution.py:32
  552.8 12.1 reduce-scatter.27.cloned.1.call-done
  566.9 24.9 %reduce-scatter.29.cloned.1.call-done = f32[256,128]{1,0:T(8,128)} async-done(((f32[1024,128]{1,0:T(8,128)}), f32[256,128]{1,0:T(8,128)}) %reduce-scatter.29.cloned.1.call-update) | async-done | bytes 131088 | tf_op jit(solution)/shard_map/reduce_scatter | solution.py:45
  592.7 12.2 all_gather.55
  605.8 109.8 %all-reduce.15.cloned.1.call-done = bf16[1024,128]{1,0:T(8,128)(2,1)} async-done(((bf16[1024,128]{1,0:T(8,128)(2,1)}), bf16[1024,128]{1,0:T(8,128)(2,1)}) %all-reduce.15.cloned.1.call-update) | async-done | bytes 262160 | tf_op jit(solution)/shard_map/psum | solution.py:9
  716.5 16.5 %all-gather.4 = bf16[1,1024,256]{2,1,0:T(8,128)(2,1)S(1)} all-gather(bf16[1,64,256]{2,1,0:T(8,128)(2,1)S(1)} %get-tuple-element.154), channel_id=6, replica_groups=mesh['row'=16,'col'=4,'rhs'=4] {'row'}, dimensions={1}, use_global_device_ids=true | all-gather | bytes 557056 | tf_op jit(solution)/shard_map/all_gather | solution.py:32
  733.0 11.8 reduce-scatter.31.cloned.1.call-done
  744.8 2.0 fusion.16
  746.9 25.0 %reduce-scatter.33.cloned.1.call-done = f32[256,128]{1,0:T(8,128)} async-done(((f32[1024,128]{1,0:T(8,128)}), f32[256,128]{1,0:T(8,128)}) %reduce-scatter.33.cloned.1.call-update) | async-done | bytes 131088 | tf_op jit(solution)/shard_map/reduce_scatter | solution.py:45
  772.8 12.2 all_gather.57
  785.8 109.8 %all-reduce.17.cloned.1.call-done = bf16[1024,128]{1,0:T(8,128)(2,1)} async-done(((bf16[1024,128]{1,0:T(8,128)(2,1)}), bf16[1024,128]{1,0:T(8,128)(2,1)}) %all-reduce.17.cloned.1.call-update) | async-done | bytes 262160 | tf_op jit(solution)/shard_map/psum | solution.py:9
  895.7 3.8 conditional.12
  895.7 3.5 fusion.70
  900.4 16.5 %all-gather.5 = bf16[1,1024,256]{2,1,0:T(8,128)(2,1)S(1)} all-gather(bf16[1,64,256]{2,1,0:T(8,128)(2,1)S(1)} %get-tuple-element.153), channel_id=7, replica_groups=mesh['row'=16,'col'=4,'rhs'=4] {'row'}, dimensions={1}, use_global_device_ids=true | all-gather | bytes 557056 | tf_op jit(solution)/shard_map/all_gather | solution.py:32
  917.0 6.3 reduce-scatter.35.cloned.1.call-done
  925.3 24.9 %reduce-scatter.37.cloned.1.call-done = f32[256,128]{1,0:T(8,128)} async-done(((f32[1024,128]{1,0:T(8,128)}), f32[256,128]{1,0:T(8,128)}) %reduce-scatter.37.cloned.1.call-update) | async-done | bytes 131088 | tf_op jit(solution)/shard_map/reduce_scatter | solution.py:45
  951.2 12.2 all_gather.59
  964.2 109.8 %all-reduce.19.cloned.1.call-done = bf16[1024,128]{1,0:T(8,128)(2,1)} async-done(((bf16[1024,128]{1,0:T(8,128)(2,1)}), bf16[1024,128]{1,0:T(8,128)(2,1)}) %all-reduce.19.cloned.1.call-update) | async-done | bytes 262160 | tf_op jit(solution)/shard_map/psum | solution.py:9
  1074.9 16.5 %all-gather.6 = bf16[1,1024,256]{2,1,0:T(8,128)(2,1)S(1)} all-gather(bf16[1,64,256]{2,1,0:T(8,128)(2,1)S(1)} %get-tuple-element.159), channel_id=8, replica_groups=mesh['row'=16,'col'=4,'rhs'=4] {'row'}, dimensions={1}, use_global_device_ids=true | all-gather | bytes 557056 | tf_op jit(solution)/shard_map/all_gather | solution.py:32
  1091.5 10.6 reduce-scatter.39.cloned.1.call-done
  1104.1 25.0 %reduce-scatter.41.cloned.1.call-done = f32[256,128]{1,0:T(8,128)} async-done(((f32[1024,128]{1,0:T(8,128)}), f32[256,128]{1,0:T(8,128)}) %reduce-scatter.41.cloned.1.call-update) | async-done | bytes 131088 | tf_op jit(solution)/shard_map/reduce_scatter | solution.py:45
  1130.0 12.2 all_gather.61
  1143.1 109.9 %all-reduce.21.cloned.1.call-done = bf16[1024,128]{1,0:T(8,128)(2,1)} async-done(((bf16[1024,128]{1,0:T(8,128)(2,1)}), bf16[1024,128]{1,0:T(8,128)(2,1)}) %all-reduce.21.cloned.1.call-update) | async-done | bytes 262160 | tf_op jit(solution)/shard_map/psum | solution.py:9
  1253.8 16.5 %all-gather.7 = bf16[1,1024,256]{2,1,0:T(8,128)(2,1)S(1)} all-gather(bf16[1,64,256]{2,1,0:T(8,128)(2,1)S(1)} %get-tuple-element.152), channel_id=9, replica_groups=mesh['row'=16,'col'=4,'rhs'=4] {'row'}, dimensions={1}, use_global_device_ids=true | all-gather | bytes 557056 | tf_op jit(solution)/shard_map/all_gather | solution.py:32
  1270.4 12.1 reduce-scatter.43.cloned.1.call-done
  1282.4 2.0 fusion.22
  1284.5 25.0 %reduce-scatter.45.cloned.1.call-done = f32[256,128]{1,0:T(8,128)} async-done(((f32[1024,128]{1,0:T(8,128)}), f32[256,128]{1,0:T(8,128)}) %reduce-scatter.45.cloned.1.call-update) | async-done | bytes 131088 | tf_op jit(solution)/shard_map/reduce_scatter | solution.py:45
  1310.4 12.2 all_gather.63
  1323.5 109.8 %all-reduce.23.cloned.1.call-done = bf16[1024,128]{1,0:T(8,128)(2,1)} async-done(((bf16[1024,128]{1,0:T(8,128)(2,1)}), bf16[1024,128]{1,0:T(8,128)(2,1)}) %all-reduce.23.cloned.1.call-update) | async-done | bytes 262160 | tf_op jit(solution)/shard_map/psum | solution.py:9
  1441.1 21.5 %reduce-scatter.47.cloned.1.call-done = bf16[512,128]{1,0:T(8,128)(2,1)} async-done(((bf16[2048,128]{1,0:T(8,128)(2,1)}), bf16[512,128]{1,0:T(8,128)(2,1)}) %reduce-scatter.47.cloned.1.call-update) | async-done | bytes 131088 | tf_op jit(solution)/shard_map/reduce_scatter | solution.py:71
  (102 shorter events, 41.3 us)
Async XLA Ops:
  7.2 46.9 %reduce-scatter.17.cloned.1.call-start = ((), (), s32[]{:S(2)}) async-start(), calls=%async_computation.16 | async-start | bytes 655360 | tf_op jit(solution)/shard_map/reduce_scatter | solution.py:45
  31.7 146.2 %all-reduce.9.cloned.1.call-start = ((), (), s32[]{:S(2)}) async-start(), calls=%async_computation.17 | async-start | bytes 524288 | tf_op jit(solution)/shard_map/psum | solution.py:9
  68.0 137.6 %reduce-scatter.19.cloned.1.call-start = ((), (), s32[]{:S(2)}) async-start(), calls=%async_computation.18 | async-start | bytes 655360 | tf_op jit(solution)/shard_map/reduce_scatter | solution.py:33
  182.4 50.3 %reduce-scatter.21.cloned.1.call-start = ((), (), s32[]{:S(2)}) async-start(), calls=%async_computation.19 | async-start | bytes 655360 | tf_op jit(solution)/shard_map/reduce_scatter | solution.py:45
  207.7 148.8 %all-reduce.11.cloned.1.call-start = ((), (), s32[]{:S(2)}) async-start(), calls=%async_computation.20 | async-start | bytes 524288 | tf_op jit(solution)/shard_map/psum | solution.py:9
  246.6 137.9 %reduce-scatter.23.cloned.1.call-start = ((), (), s32[]{:S(2)}) async-start(), calls=%async_computation.21 | async-start | bytes 655360 | tf_op jit(solution)/shard_map/reduce_scatter | solution.py:33
  357.3 54.2 %reduce-scatter.25.cloned.1.call-start = ((), (), s32[]{:S(2)}) async-start(), calls=%async_computation.22 | async-start | bytes 655360 | tf_op jit(solution)/shard_map/reduce_scatter | solution.py:45
  386.5 148.8 %all-reduce.13.cloned.1.call-start = ((), (), s32[]{:S(2)}) async-start(), calls=%async_computation.23 | async-start | bytes 524288 | tf_op jit(solution)/shard_map/psum | solution.py:9
  425.4 139.4 %reduce-scatter.27.cloned.1.call-start = ((), (), s32[]{:S(2)}) async-start(), calls=%async_computation.24 | async-start | bytes 655360 | tf_op jit(solution)/shard_map/reduce_scatter | solution.py:33
  536.2 55.6 %reduce-scatter.29.cloned.1.call-start = ((), (), s32[]{:S(2)}) async-start(), calls=%async_computation.25 | async-start | bytes 655360 | tf_op jit(solution)/shard_map/reduce_scatter | solution.py:45
  566.9 148.7 %all-reduce.15.cloned.1.call-start = ((), (), s32[]{:S(2)}) async-start(), calls=%async_computation.26 | async-start | bytes 524288 | tf_op jit(solution)/shard_map/psum | solution.py:9
  605.7 139.1 %reduce-scatter.31.cloned.1.call-start = ((), (), s32[]{:S(2)}) async-start(), calls=%async_computation.27 | async-start | bytes 655360 | tf_op jit(solution)/shard_map/reduce_scatter | solution.py:33
  716.4 55.4 %reduce-scatter.33.cloned.1.call-start = ((), (), s32[]{:S(2)}) async-start(), calls=%async_computation.28 | async-start | bytes 655360 | tf_op jit(solution)/shard_map/reduce_scatter | solution.py:45
  746.8 148.8 %all-reduce.17.cloned.1.call-start = ((), (), s32[]{:S(2)}) async-start(), calls=%async_computation.29 | async-start | bytes 524288 | tf_op jit(solution)/shard_map/psum | solution.py:9
  785.8 137.5 %reduce-scatter.35.cloned.1.call-start = ((), (), s32[]{:S(2)}) async-start(), calls=%async_computation.30 | async-start | bytes 655360 | tf_op jit(solution)/shard_map/reduce_scatter | solution.py:33
  900.4 49.9 %reduce-scatter.37.cloned.1.call-start = ((), (), s32[]{:S(2)}) async-start(), calls=%async_computation.31 | async-start | bytes 655360 | tf_op jit(solution)/shard_map/reduce_scatter | solution.py:45
  925.3 148.8 %all-reduce.19.cloned.1.call-start = ((), (), s32[]{:S(2)}) async-start(), calls=%async_computation.32 | async-start | bytes 524288 | tf_op jit(solution)/shard_map/psum | solution.py:9
  964.2 137.9 %reduce-scatter.39.cloned.1.call-start = ((), (), s32[]{:S(2)}) async-start(), calls=%async_computation.33 | async-start | bytes 655360 | tf_op jit(solution)/shard_map/reduce_scatter | solution.py:33
  1074.9 54.2 %reduce-scatter.41.cloned.1.call-start = ((), (), s32[]{:S(2)}) async-start(), calls=%async_computation.34 | async-start | bytes 655360 | tf_op jit(solution)/shard_map/reduce_scatter | solution.py:45
  1104.0 148.9 %all-reduce.21.cloned.1.call-start = ((), (), s32[]{:S(2)}) async-start(), calls=%async_computation.35 | async-start | bytes 524288 | tf_op jit(solution)/shard_map/psum | solution.py:9
  1143.0 139.4 %reduce-scatter.43.cloned.1.call-start = ((), (), s32[]{:S(2)}) async-start(), calls=%async_computation.36 | async-start | bytes 655360 | tf_op jit(solution)/shard_map/reduce_scatter | solution.py:33
  1253.8 55.7 %reduce-scatter.45.cloned.1.call-start = ((), (), s32[]{:S(2)}) async-start(), calls=%async_computation.37 | async-start | bytes 655360 | tf_op jit(solution)/shard_map/reduce_scatter | solution.py:45
  1284.5 148.9 %all-reduce.23.cloned.1.call-start = ((), (), s32[]{:S(2)}) async-start(), calls=%async_computation.38 | async-start | bytes 524288 | tf_op jit(solution)/shard_map/psum | solution.py:9
  1323.4 139.1 %reduce-scatter.47.cloned.1.call-start = ((), (), s32[]{:S(2)}) async-start(), calls=%async_computation.39 | async-start | bytes 655360 | tf_op jit(solution)/shard_map/reduce_scatter | solution.py:71
  1441.1 23.2 %copy-start = (bf16[8,256,128]{2,1,0:T(8,128)(2,1)}, bf16[8,256,128]{2,1,0:T(8,128)(2,1)S(1)}, u32[]{:S(2)}) copy-start(bf16[8,256,128]{2,1,0:T(8,128)(2,1)S(1)} %bitcast_dynamic-update-slice_fusion) | copy-start | bytes 1572868
Sparse Core Ops, SparseCore 0:
  31.9 22.2 reduce-scatter.16
  68.1 109.7 all-reduce.8
  182.5 23.0 reduce-scatter.18
  208.6 24.0 reduce-scatter.20
  246.7 109.7 all-reduce.10
  359.4 25.0 reduce-scatter.22
  387.6 23.9 reduce-scatter.24
  425.6 109.7 all-reduce.12
  538.5 26.3 reduce-scatter.26
  567.8 23.9 reduce-scatter.28
  605.8 109.7 all-reduce.14
  718.5 26.2 reduce-scatter.30
  747.9 23.9 reduce-scatter.32
  785.9 109.7 all-reduce.16
  900.5 22.7 reduce-scatter.34
  926.2 23.9 reduce-scatter.36
  964.3 109.7 all-reduce.18
  1077.0 25.0 reduce-scatter.38
  1105.1 23.9 reduce-scatter.40
  1143.1 109.7 all-reduce.20
  1256.0 26.3 reduce-scatter.42
  1285.5 23.9 reduce-scatter.44
  1323.5 109.7 all-reduce.22
  1435.7 26.8 reduce-scatter.46
where the time goes:
time: 1470 us
  waiting for transfers between devices  1160 us (79%)
  blocking collectives  235 us (16%)
  matrix products  22.1 us (2%)
  local copies, waits for them, and re-layouts  20.6 us (1%)
  other arithmetic  16.2 us (1%)
    psum x8, waiting for transfers between devices, from_root(): return lax.psum(kept, axis)  873 us
    reduce_scatter x8, waiting for transfers between devices, shards(): lax.psum_scatter(solve_term(jnp.int32(0), lax.axis_size('col') * part_row...  197 us
    all_gather x8, blocking collectives, shards(): lax.all_gather(inverses[block], 'row', axis=0, tiled=True)  137 us
    all_gather x8, blocking collectives, shards(): solved_full = lax.all_gather(solved_rows, 'col', axis=0, tiled=True)  98 us
    reduce_scatter x7, waiting for transfers between devices, shards(): lax.psum_scatter(partial_value[slot_index], 'col', scatter_dimension=0, t...  69.9 us
  transfers between devices with their start and end apart: 24, of which 24 were waited for; matrix products, arithmetic and copies ran while one was open for 1% of the time, Pallas kernels for 0%

commit v1 on v0

--- a/solution.py
+++ b/solution.py
@@ -6,7 +6,7 @@
 
 def from_root(value, axis, source):
     kept = jnp.where(lax.axis_index(axis) == source, value, 0).astype(value.dtype)
-    return lax.psum(kept, axis)
+    return jnp.sum(lax.all_gather(kept, axis), axis=0)
 
 
 def shards(factor, samples, inverses):

time: 1470 us -> 935 us (0.64)
  waiting for transfers between devices: 1160 us -> 597 us
  other arithmetic: 16.2 us -> 40.4 us
    psum x8 -> x0, waiting for transfers between devices: 873 us -> none  [from_root(): return lax.psum(kept, axis)]
    all_gather x0 -> x8, waiting for transfers between devices: none -> 328 us  [from_root(): return jnp.sum(lax.all_gather(kept, axis), axis=0)]
    reduce_sum x0 -> x8, other arithmetic: none -> 24.2 us  [from_root(): return jnp.sum(lax.all_gather(kept, axis), axis=0)]
    reduce_scatter x7, waiting for transfers between devices: 69.9 us -> 47 us  [shards(): lax.psum_scatter(partial_value[slot_index], 'col', scatter_dimension=0, t...]
where the time goes in v1:
time: 935 us; the launch traced here: 934 us
  waiting for transfers between devices  597 us (64%)
  blocking collectives  243 us (26%)
  other arithmetic  40.4 us (4%)
  matrix products  22 us (2%)
  local copies, waits for them, and re-layouts  15.5 us (2%)
  between operations  14.6 us (2%)
    all_gather x8, waiting for transfers between devices, from_root(): return jnp.sum(lax.all_gather(kept, axis), axis=0)  328 us
    reduce_scatter x8, waiting for transfers between devices, shards(): lax.psum_scatter(solve_term(jnp.int32(0), lax.axis_size('col') * part_row...  197 us
    all_gather x8, blocking collectives, shards(): lax.all_gather(inverses[block], 'row', axis=0, tiled=True)  145 us
    all_gather x8, blocking collectives, shards(): solved_full = lax.all_gather(solved_rows, 'col', axis=0, tiled=True)  98 us
    reduce_scatter x7, waiting for transfers between devices, shards(): lax.psum_scatter(partial_value[slot_index], 'col', scatter_dimension=0, t...  47 us
    reduce_scatter x1, waiting for transfers between devices, shards(): lax.psum_scatter(partial_value.reshape(row_slots * width, sample_cols).as...  24.5 us
    reduce_sum x8, other arithmetic, from_root(): return jnp.sum(lax.all_gather(kept, axis), axis=0)  24.2 us
  transfers between devices with their start and end apart: 24, of which 24 were waited for; matrix products, arithmetic and copies ran while one was open for 1% of the time, Pallas kernels for 0%

profile of v1, /device:TPU:8, one launch (start us, length us, event | category | flops | bytes accessed | tf_op | source)
XLA Modules:
  0.0 933.7 jit_solution(4029915453405243077)
XLA Ops:
  8.1 21.4 %all-gather = bf16[1,1024,256]{2,1,0:T(8,128)(2,1)S(1)} all-gather(bf16[1,64,256]{2,1,0:T(8,128)(2,1)S(1)} %get-tuple-element.158), channel_id=2, replica_groups=mesh['row'=16,'col'=4,'rhs'=4] {'row'}, dimensions={1}, use_global_device_ids=true | all-gather | bytes 557056 | tf_op jit(solution)/shard_map/all_gather | solution.py:32
  31.8 22.3 %reduce-scatter.17.cloned.1.call-done = f32[256,128]{1,0:T(8,128)} async-done(((f32[1024,128]{1,0:T(8,128)}), f32[256,128]{1,0:T(8,128)}) %reduce-scatter.17.cloned.1.call-update) | async-done | bytes 131088 | tf_op jit(solution)/shard_map/reduce_scatter | solution.py:45
  55.0 12.2 %all_gather.97 = bf16[1024,128]{1,0:T(8,128)(2,1)S(1)} all-gather(bf16[256,128]{1,0:T(8,128)(2,1)S(1)} %convert_element_type.99), channel_id=1, replica_groups=mesh['row'=16,'col'=4,'rhs'=4] {'col'}, dimensions={0}, use_global_device_ids=true | all-gather | bytes 327680 | tf_op jit(solution)/shard_map/all_gather | solution.py:51
  68.0 5.9 fusion.64
  74.0 35.8 %all-gather.25.cloned.1.call-done = bf16[16384,128]{1,0:T(8,128)(2,1)} async-done(((bf16[1024,128]{1,0:T(8,128)(2,1)}), bf16[16384,128]{1,0:T(8,128)(2,1)}) %all-gather.25.cloned.1.call-update) | async-done | bytes 4194320 | tf_op jit(solution)/shard_map/all_gather | solution.py:9
  109.8 2.9 reduce_sum.96
  112.7 3.6 conditional.8
  112.7 3.5 fusion.66
  117.2 17.6 %all-gather.2 = bf16[1,1024,256]{2,1,0:T(8,128)(2,1)S(1)} all-gather(bf16[1,64,256]{2,1,0:T(8,128)(2,1)S(1)} %get-tuple-element.157), channel_id=4, replica_groups=mesh['row'=16,'col'=4,'rhs'=4] {'row'}, dimensions={1}, use_global_device_ids=true | all-gather | bytes 557056 | tf_op jit(solution)/shard_map/all_gather | solution.py:32
  139.6 25.0 %reduce-scatter.21.cloned.1.call-done = f32[256,128]{1,0:T(8,128)} async-done(((f32[1024,128]{1,0:T(8,128)}), f32[256,128]{1,0:T(8,128)}) %reduce-scatter.21.cloned.1.call-update) | async-done | bytes 131088 | tf_op jit(solution)/shard_map/reduce_scatter | solution.py:45
  165.5 12.2 %all_gather.101 = bf16[1024,128]{1,0:T(8,128)(2,1)S(1)} all-gather(bf16[256,128]{1,0:T(8,128)(2,1)S(1)} %convert_element_type.102), channel_id=1, replica_groups=mesh['row'=16,'col'=4,'rhs'=4] {'col'}, dimensions={0}, use_global_device_ids=true | all-gather | bytes 327680 | tf_op jit(solution)/shard_map/all_gather | solution.py:51
  178.5 41.7 %all-gather.27.cloned.1.call-done = bf16[16384,128]{1,0:T(8,128)(2,1)} async-done(((bf16[1024,128]{1,0:T(8,128)(2,1)}), bf16[16384,128]{1,0:T(8,128)(2,1)}) %all-gather.27.cloned.1.call-update) | async-done | bytes 4194320 | tf_op jit(solution)/shard_map/all_gather | solution.py:9
  220.2 2.9 reduce_sum.97
  224.0 17.6 %all-gather.4 = bf16[1,1024,256]{2,1,0:T(8,128)(2,1)S(1)} all-gather(bf16[1,64,256]{2,1,0:T(8,128)(2,1)S(1)} %get-tuple-element.156), channel_id=6, replica_groups=mesh['row'=16,'col'=4,'rhs'=4] {'row'}, dimensions={1}, use_global_device_ids=true | all-gather | bytes 557056 | tf_op jit(solution)/shard_map/all_gather | solution.py:32
  241.6 7.5 reduce-scatter.23.cloned.1.call-done
  251.2 25.0 %reduce-scatter.25.cloned.1.call-done = f32[256,128]{1,0:T(8,128)} async-done(((f32[1024,128]{1,0:T(8,128)}), f32[256,128]{1,0:T(8,128)}) %reduce-scatter.25.cloned.1.call-update) | async-done | bytes 131088 | tf_op jit(solution)/shard_map/reduce_scatter | solution.py:45
  277.1 12.2 %all_gather.105 = bf16[1024,128]{1,0:T(8,128)(2,1)S(1)} all-gather(bf16[256,128]{1,0:T(8,128)(2,1)S(1)} %convert_element_type.105), channel_id=1, replica_groups=mesh['row'=16,'col'=4,'rhs'=4] {'col'}, dimensions={0}, use_global_device_ids=true | all-gather | bytes 327680 | tf_op jit(solution)/shard_map/all_gather | solution.py:51
  290.2 41.8 %all-gather.29.cloned.1.call-done = bf16[16384,128]{1,0:T(8,128)(2,1)} async-done(((bf16[1024,128]{1,0:T(8,128)(2,1)}), bf16[16384,128]{1,0:T(8,128)(2,1)}) %all-gather.29.cloned.1.call-update) | async-done | bytes 4194320 | tf_op jit(solution)/shard_map/all_gather | solution.py:9
  335.7 17.6 %all-gather.6 = bf16[1,1024,256]{2,1,0:T(8,128)(2,1)S(1)} all-gather(bf16[1,64,256]{2,1,0:T(8,128)(2,1)S(1)} %get-tuple-element.155), channel_id=8, replica_groups=mesh['row'=16,'col'=4,'rhs'=4] {'row'}, dimensions={1}, use_global_device_ids=true | all-gather | bytes 557056 | tf_op jit(solution)/shard_map/all_gather | solution.py:32
  353.3 9.0 reduce-scatter.27.cloned.1.call-done
  364.4 24.9 %reduce-scatter.29.cloned.1.call-done = f32[256,128]{1,0:T(8,128)} async-done(((f32[1024,128]{1,0:T(8,128)}), f32[256,128]{1,0:T(8,128)}) %reduce-scatter.29.cloned.1.call-update) | async-done | bytes 131088 | tf_op jit(solution)/shard_map/reduce_scatter | solution.py:45
  390.2 12.2 %all_gather.109 = bf16[1024,128]{1,0:T(8,128)(2,1)S(1)} all-gather(bf16[256,128]{1,0:T(8,128)(2,1)S(1)} %convert_element_type.108), channel_id=1, replica_groups=mesh['row'=16,'col'=4,'rhs'=4] {'col'}, dimensions={0}, use_global_device_ids=true | all-gather | bytes 327680 | tf_op jit(solution)/shard_map/all_gather | solution.py:51
  403.2 41.8 %all-gather.31.cloned.1.call-done = bf16[16384,128]{1,0:T(8,128)(2,1)} async-done(((bf16[1024,128]{1,0:T(8,128)(2,1)}), bf16[16384,128]{1,0:T(8,128)(2,1)}) %all-gather.31.cloned.1.call-update) | async-done | bytes 4194320 | tf_op jit(solution)/shard_map/all_gather | solution.py:9
  448.8 17.8 %all-gather.8 = bf16[1,1024,256]{2,1,0:T(8,128)(2,1)S(1)} all-gather(bf16[1,64,256]{2,1,0:T(8,128)(2,1)S(1)} %get-tuple-element.154), channel_id=10, replica_groups=mesh['row'=16,'col'=4,'rhs'=4] {'row'}, dimensions={1}, use_global_device_ids=true | all-gather | bytes 557056 | tf_op jit(solution)/shard_map/all_gather | solution.py:32
  466.6 8.6 reduce-scatter.31.cloned.1.call-done
  477.2 25.0 %reduce-scatter.33.cloned.1.call-done = f32[256,128]{1,0:T(8,128)} async-done(((f32[1024,128]{1,0:T(8,128)}), f32[256,128]{1,0:T(8,128)}) %reduce-scatter.33.cloned.1.call-update) | async-done | bytes 131088 | tf_op jit(solution)/shard_map/reduce_scatter | solution.py:45
  503.1 12.2 %all_gather.113 = bf16[1024,128]{1,0:T(8,128)(2,1)S(1)} all-gather(bf16[256,128]{1,0:T(8,128)(2,1)S(1)} %convert_element_type.111), channel_id=1, replica_groups=mesh['row'=16,'col'=4,'rhs'=4] {'col'}, dimensions={0}, use_global_device_ids=true | all-gather | bytes 327680 | tf_op jit(solution)/shard_map/all_gather | solution.py:51
  516.1 41.7 %all-gather.33.cloned.1.call-done = bf16[16384,128]{1,0:T(8,128)(2,1)} async-done(((bf16[1024,128]{1,0:T(8,128)(2,1)}), bf16[16384,128]{1,0:T(8,128)(2,1)}) %all-gather.33.cloned.1.call-update) | async-done | bytes 4194320 | tf_op jit(solution)/shard_map/all_gather | solution.py:9
  557.9 2.9 reduce_sum.100
  560.7 3.8 conditional.12
  560.8 3.5 fusion.70
  565.5 17.6 %all-gather.10 = bf16[1,1024,256]{2,1,0:T(8,128)(2,1)S(1)} all-gather(bf16[1,64,256]{2,1,0:T(8,128)(2,1)S(1)} %get-tuple-element.153), channel_id=12, replica_groups=mesh['row'=16,'col'=4,'rhs'=4] {'row'}, dimensions={1}, use_global_device_ids=true | all-gather | bytes 557056 | tf_op jit(solution)/shard_map/all_gather | solution.py:32
  587.8 25.1 %reduce-scatter.37.cloned.1.call-done = f32[256,128]{1,0:T(8,128)} async-done(((f32[1024,128]{1,0:T(8,128)}), f32[256,128]{1,0:T(8,128)}) %reduce-scatter.37.cloned.1.call-update) | async-done | bytes 131088 | tf_op jit(solution)/shard_map/reduce_scatter | solution.py:45
  613.8 12.2 %all_gather.117 = bf16[1024,128]{1,0:T(8,128)(2,1)S(1)} all-gather(bf16[256,128]{1,0:T(8,128)(2,1)S(1)} %convert_element_type.113), channel_id=1, replica_groups=mesh['row'=16,'col'=4,'rhs'=4] {'col'}, dimensions={0}, use_global_device_ids=true | all-gather | bytes 327680 | tf_op jit(solution)/shard_map/all_gather | solution.py:51
  626.9 41.9 %all-gather.35.cloned.1.call-done = bf16[16384,128]{1,0:T(8,128)(2,1)} async-done(((bf16[1024,128]{1,0:T(8,128)(2,1)}), bf16[16384,128]{1,0:T(8,128)(2,1)}) %all-gather.35.cloned.1.call-update) | async-done | bytes 4194320 | tf_op jit(solution)/shard_map/all_gather | solution.py:9
  668.7 3.5 reduce_sum.101
  673.2 17.6 %all-gather.12 = bf16[1,1024,256]{2,1,0:T(8,128)(2,1)S(1)} all-gather(bf16[1,64,256]{2,1,0:T(8,128)(2,1)S(1)} %get-tuple-element.159), channel_id=14, replica_groups=mesh['row'=16,'col'=4,'rhs'=4] {'row'}, dimensions={1}, use_global_device_ids=true | all-gather | bytes 557056 | tf_op jit(solution)/shard_map/all_gather | solution.py:32
  690.8 7.5 reduce-scatter.39.cloned.1.call-done
  700.4 25.0 %reduce-scatter.41.cloned.1.call-done = f32[256,128]{1,0:T(8,128)} async-done(((f32[1024,128]{1,0:T(8,128)}), f32[256,128]{1,0:T(8,128)}) %reduce-scatter.41.cloned.1.call-update) | async-done | bytes 131088 | tf_op jit(solution)/shard_map/reduce_scatter | solution.py:45
  726.3 12.2 %all_gather.121 = bf16[1024,128]{1,0:T(8,128)(2,1)S(1)} all-gather(bf16[256,128]{1,0:T(8,128)(2,1)S(1)} %convert_element_type.115), channel_id=1, replica_groups=mesh['row'=16,'col'=4,'rhs'=4] {'col'}, dimensions={0}, use_global_device_ids=true | all-gather | bytes 327680 | tf_op jit(solution)/shard_map/all_gather | solution.py:51
  739.3 41.7 %all-gather.37.cloned.1.call-done = bf16[16384,128]{1,0:T(8,128)(2,1)} async-done(((bf16[1024,128]{1,0:T(8,128)(2,1)}), bf16[16384,128]{1,0:T(8,128)(2,1)}) %all-gather.37.cloned.1.call-update) | async-done | bytes 4194320 | tf_op jit(solution)/shard_map/all_gather | solution.py:9
  781.1 3.5 reduce_sum.102
  785.5 17.6 %all-gather.14 = bf16[1,1024,256]{2,1,0:T(8,128)(2,1)S(1)} all-gather(bf16[1,64,256]{2,1,0:T(8,128)(2,1)S(1)} %get-tuple-element.152), channel_id=16, replica_groups=mesh['row'=16,'col'=4,'rhs'=4] {'row'}, dimensions={1}, use_global_device_ids=true | all-gather | bytes 557056 | tf_op jit(solution)/shard_map/all_gather | solution.py:32
  803.1 9.0 reduce-scatter.43.cloned.1.call-done
  814.3 25.0 %reduce-scatter.45.cloned.1.call-done = f32[256,128]{1,0:T(8,128)} async-done(((f32[1024,128]{1,0:T(8,128)}), f32[256,128]{1,0:T(8,128)}) %reduce-scatter.45.cloned.1.call-update) | async-done | bytes 131088 | tf_op jit(solution)/shard_map/reduce_scatter | solution.py:45
  840.2 12.2 %all_gather.125 = bf16[1024,128]{1,0:T(8,128)(2,1)S(1)} all-gather(bf16[256,128]{1,0:T(8,128)(2,1)S(1)} %convert_element_type.117), channel_id=1, replica_groups=mesh['row'=16,'col'=4,'rhs'=4] {'col'}, dimensions={0}, use_global_device_ids=true | all-gather | bytes 327680 | tf_op jit(solution)/shard_map/all_gather | solution.py:51
  853.2 41.7 %all-gather.39.cloned.1.call-done = bf16[16384,128]{1,0:T(8,128)(2,1)} async-done(((bf16[1024,128]{1,0:T(8,128)(2,1)}), bf16[16384,128]{1,0:T(8,128)(2,1)}) %all-gather.39.cloned.1.call-update) | async-done | bytes 4194320 | tf_op jit(solution)/shard_map/all_gather | solution.py:9
  900.6 24.5 %reduce-scatter.47.cloned.1.call-done = bf16[512,128]{1,0:T(8,128)(2,1)} async-done(((bf16[2048,128]{1,0:T(8,128)(2,1)}), bf16[512,128]{1,0:T(8,128)(2,1)}) %reduce-scatter.47.cloned.1.call-update) | async-done | bytes 131088 | tf_op jit(solution)/shard_map/reduce_scatter | solution.py:71
  (110 shorter events, 56.2 us)
Async XLA Ops:
  7.2 46.9 %reduce-scatter.17.cloned.1.call-start = ((), (), s32[]{:S(2)}) async-start(), calls=%async_computation.16 | async-start | bytes 655360 | tf_op jit(solution)/shard_map/reduce_scatter | solution.py:45
  31.7 78.1 %all-gather.25.cloned.1.call-start = ((), (), s32[]{:S(2)}) async-start(), calls=%async_computation.32 | async-start | bytes 4456448 | tf_op jit(solution)/shard_map/all_gather | solution.py:9
  68.0 69.5 %reduce-scatter.19.cloned.1.call-start = ((), (), s32[]{:S(2)}) async-start(), calls=%async_computation.17 | async-start | bytes 655360 | tf_op jit(solution)/shard_map/reduce_scatter | solution.py:33
  117.2 47.4 %reduce-scatter.21.cloned.1.call-start = ((), (), s32[]{:S(2)}) async-start(), calls=%async_computation.18 | async-start | bytes 655360 | tf_op jit(solution)/shard_map/reduce_scatter | solution.py:45
  139.5 80.7 %all-gather.27.cloned.1.call-start = ((), (), s32[]{:S(2)}) async-start(), calls=%async_computation.33 | async-start | bytes 4456448 | tf_op jit(solution)/shard_map/all_gather | solution.py:9
  178.5 70.7 %reduce-scatter.23.cloned.1.call-start = ((), (), s32[]{:S(2)}) async-start(), calls=%async_computation.19 | async-start | bytes 655360 | tf_op jit(solution)/shard_map/reduce_scatter | solution.py:33
  224.0 52.2 %reduce-scatter.25.cloned.1.call-start = ((), (), s32[]{:S(2)}) async-start(), calls=%async_computation.20 | async-start | bytes 655360 | tf_op jit(solution)/shard_map/reduce_scatter | solution.py:45
  251.2 80.8 %all-gather.29.cloned.1.call-start = ((), (), s32[]{:S(2)}) async-start(), calls=%async_computation.34 | async-start | bytes 4456448 | tf_op jit(solution)/shard_map/all_gather | solution.py:9
  290.1 72.2 %reduce-scatter.27.cloned.1.call-start = ((), (), s32[]{:S(2)}) async-start(), calls=%async_computation.21 | async-start | bytes 655360 | tf_op jit(solution)/shard_map/reduce_scatter | solution.py:33
  335.7 53.6 %reduce-scatter.29.cloned.1.call-start = ((), (), s32[]{:S(2)}) async-start(), calls=%async_computation.22 | async-start | bytes 655360 | tf_op jit(solution)/shard_map/reduce_scatter | solution.py:45
  364.4 80.6 %all-gather.31.cloned.1.call-start = ((), (), s32[]{:S(2)}) async-start(), calls=%async_computation.35 | async-start | bytes 4456448 | tf_op jit(solution)/shard_map/all_gather | solution.py:9
  403.2 72.0 %reduce-scatter.31.cloned.1.call-start = ((), (), s32[]{:S(2)}) async-start(), calls=%async_computation.23 | async-start | bytes 655360 | tf_op jit(solution)/shard_map/reduce_scatter | solution.py:33
  448.7 53.5 %reduce-scatter.33.cloned.1.call-start = ((), (), s32[]{:S(2)}) async-start(), calls=%async_computation.24 | async-start | bytes 655360 | tf_op jit(solution)/shard_map/reduce_scatter | solution.py:45
  477.1 80.7 %all-gather.33.cloned.1.call-start = ((), (), s32[]{:S(2)}) async-start(), calls=%async_computation.36 | async-start | bytes 4456448 | tf_op jit(solution)/shard_map/all_gather | solution.py:9
  516.1 69.7 %reduce-scatter.35.cloned.1.call-start = ((), (), s32[]{:S(2)}) async-start(), calls=%async_computation.25 | async-start | bytes 655360 | tf_op jit(solution)/shard_map/reduce_scatter | solution.py:33
  565.4 47.5 %reduce-scatter.37.cloned.1.call-start = ((), (), s32[]{:S(2)}) async-start(), calls=%async_computation.26 | async-start | bytes 655360 | tf_op jit(solution)/shard_map/reduce_scatter | solution.py:45
  587.8 81.0 %all-gather.35.cloned.1.call-start = ((), (), s32[]{:S(2)}) async-start(), calls=%async_computation.37 | async-start | bytes 4456448 | tf_op jit(solution)/shard_map/all_gather | solution.py:9
  626.8 71.5 %reduce-scatter.39.cloned.1.call-start = ((), (), s32[]{:S(2)}) async-start(), calls=%async_computation.27 | async-start | bytes 655360 | tf_op jit(solution)/shard_map/reduce_scatter | solution.py:33
  673.1 52.3 %reduce-scatter.41.cloned.1.call-start = ((), (), s32[]{:S(2)}) async-start(), calls=%async_computation.28 | async-start | bytes 655360 | tf_op jit(solution)/shard_map/reduce_scatter | solution.py:45
  700.3 80.7 %all-gather.37.cloned.1.call-start = ((), (), s32[]{:S(2)}) async-start(), calls=%async_computation.38 | async-start | bytes 4456448 | tf_op jit(solution)/shard_map/all_gather | solution.py:9
  739.3 72.9 %reduce-scatter.43.cloned.1.call-start = ((), (), s32[]{:S(2)}) async-start(), calls=%async_computation.29 | async-start | bytes 655360 | tf_op jit(solution)/shard_map/reduce_scatter | solution.py:33
  785.5 53.8 %reduce-scatter.45.cloned.1.call-start = ((), (), s32[]{:S(2)}) async-start(), calls=%async_computation.30 | async-start | bytes 655360 | tf_op jit(solution)/shard_map/reduce_scatter | solution.py:45
  814.2 80.8 %all-gather.39.cloned.1.call-start = ((), (), s32[]{:S(2)}) async-start(), calls=%async_computation.39 | async-start | bytes 4456448 | tf_op jit(solution)/shard_map/all_gather | solution.py:9
  853.2 71.9 %reduce-scatter.47.cloned.1.call-start = ((), (), s32[]{:S(2)}) async-start(), calls=%async_computation.31 | async-start | bytes 655360 | tf_op jit(solution)/shard_map/reduce_scatter | solution.py:71
  900.6 26.2 %copy-start = (bf16[8,256,128]{2,1,0:T(8,128)(2,1)}, bf16[8,256,128]{2,1,0:T(8,128)(2,1)S(1)}, u32[]{:S(2)}) copy-start(bf16[8,256,128]{2,1,0:T(8,128)(2,1)S(1)} %bitcast_dynamic-update-slice_fusion) | copy-start | bytes 1572868
Sparse Core Ops, SparseCore 0:
  31.9 22.1 reduce-scatter.16
  68.1 41.6 all-gather.24
  117.3 20.1 reduce-scatter.18
  140.5 24.0 reduce-scatter.20
  178.6 41.6 all-gather.26
  224.1 25.0 reduce-scatter.22
  252.2 23.9 reduce-scatter.24
  290.2 41.6 all-gather.28
  335.8 26.5 reduce-scatter.26
  365.3 23.9 reduce-scatter.28
  403.3 41.6 all-gather.30
  448.8 26.2 reduce-scatter.30
  478.2 23.9 reduce-scatter.32
  516.2 41.6 all-gather.32
  565.5 20.1 reduce-scatter.34
  588.7 24.1 reduce-scatter.36
  626.9 41.7 all-gather.34
  673.2 25.0 reduce-scatter.38
  701.4 23.9 reduce-scatter.40
  739.4 41.6 all-gather.36
  785.6 26.5 reduce-scatter.42
  815.3 23.9 reduce-scatter.44
  853.3 41.6 all-gather.38
  898.9 26.2 reduce-scatter.46
